TPU v7x, 32 devices: a whole 2x2x4 slice. The times are simulated.
32 devices in a mesh: row: 8 (over z, x), col: 4 (over y, core).
Axes of the slice: x: 2, y: 2, z: 4, core: 2. Of those that a mesh axis runs over, the one named last changes fastest.
Arguments:
- field: bfloat16 [1, 64, 512, 512], P(None, None, 'row', 'col'), may hold values from -6 to 6
- x_weight: float32 [2, 2, 12, 64, 64], replicated, may hold values from -2 to 2
- y_weight: float32 [2, 2, 12, 64, 64], replicated, may hold values from -2 to 2
- up_weight: bfloat16 [2, 256, 64], replicated, may hold values from -0.75 to 0.75
- up_bias: float32 [2, 256], replicated, may hold values from -3 to 3
- down_weight: bfloat16 [2, 64, 256], replicated, may hold values from -0.375 to 0.375
Outputs:
- result: bfloat16 [1, 64, 512, 512], P(None, None, 'row', 'col')
All inputs are finite; a program needn't handle non-finite values.
Results may differ from a plain program's by a relative error of at most 0.025.
Values may be sent and summed in bfloat16 or wider, within the bound.
A program may use at most 64 MiB of HBM per device.

v0:
```python
import functools
import math

import jax
import jax.numpy as jnp
from jax import lax
from jax.experimental import pallas as pl
from jax.experimental.pallas import tpu as pltpu
from jax.sharding import PartitionSpec as P

MODES = 12
LAYERS = 2
MESH = pl.DeviceIdType.MESH
VMEM = pltpu.VMEM


def tables(total, start, count):
    pos = start + jnp.arange(count, dtype=jnp.int32)
    kays = jnp.arange(MODES, dtype=jnp.int32)
    phase = kays[:, None] * pos[None, :] % total
    angle = phase.astype(jnp.float32) * (2.0 * math.pi / total)
    both = jnp.stack([jnp.cos(angle), -jnp.sin(angle)], axis=1)
    factor = (jnp.where(kays == 0, 1.0, 2.0) / total).astype(jnp.float32)[:, None, None]
    forward = both.astype(jnp.bfloat16).reshape(2 * MODES, count)
    inverse = (both * factor).astype(jnp.bfloat16).reshape(2 * MODES, count)
    return forward, inverse


def exchange_kernel(
    nr, nc, x_in, y_in, wx, wy, x_out, y_out, x_got, y_got, x_mat, y_mat,
    xs_send, xs_recv, ys_send, ys_recv, xg_send, xg_recv, yg_send, yg_recv,
):
    row = lax.axis_index("row")
    col = lax.axis_index("col")

    def row_peer(d):
        return (lax.rem(row + d, nr), col)

    def col_peer(d):
        return (row, lax.rem(col + d, nc))

    barrier = pltpu.get_barrier_semaphore()
    for d in range(1, nr):
        pl.semaphore_signal(barrier, inc=1, device_id=row_peer(d), device_id_type=MESH)
    for d in range(1, nc):
        pl.semaphore_signal(barrier, inc=1, device_id=col_peer(d), device_id_type=MESH)
    pl.semaphore_wait(barrier, nr + nc - 2)

    def copy(src, dst, send, recv, d, peer):
        made = pltpu.make_async_remote_copy(
            src_ref=src, dst_ref=dst, send_sem=send.at[d], recv_sem=recv.at[d],
            device_id=peer, device_id_type=MESH,
        )
        made.start()
        return made

    y_scatter = [
        copy(y_in.at[col_peer(d)[1]], y_got.at[d], ys_send, ys_recv, d, col_peer(d))
        for d in range(1, nc)
    ]
    x_scatter = [
        copy(x_in.at[row_peer(d)[0]], x_got.at[d], xs_send, xs_recv, d, row_peer(d))
        for d in range(1, nr)
    ]

    for w, mat in ((wy, y_mat), (wx, x_mat)):
        for k in range(MODES):
            real = w[0, k].astype(jnp.bfloat16)
            imag = w[1, k].astype(jnp.bfloat16)
            top = jnp.concatenate([real, imag], axis=1)
            bottom = jnp.concatenate([-imag, real], axis=1)
            mat[k] = jnp.concatenate([top, bottom], axis=0)

    def mix(own, first, got, n, mat, out):
        width = mat.shape[1]
        for k in range(MODES):
            lanes = pl.ds(k * width, width)
            total = first[own, :, lanes].astype(jnp.float32)
            for d in range(1, n):
                total = total + got[d, :, lanes].astype(jnp.float32)
            out[own, :, lanes] = jnp.dot(
                total.astype(jnp.bfloat16), mat[k], preferred_element_type=jnp.float32
            ).astype(jnp.bfloat16)

    for made in y_scatter:
        made.wait()
    mix(col, y_in, y_got, nc, y_mat, y_out)
    y_gather = [
        copy(y_out.at[col], y_out.at[col], yg_send, yg_recv, d, col_peer(d))
        for d in range(1, nc)
    ]
    for made in x_scatter:
        made.wait()
    mix(row, x_in, x_got, nr, x_mat, x_out)
    x_gather = [
        copy(x_out.at[row], x_out.at[row], xg_send, xg_recv, d, row_peer(d))
        for d in range(1, nr)
    ]
    for made in y_gather + x_gather:
        made.wait()


def exchange(x_part, y_part, wx, wy):
    nr, nc = lax.axis_size("row"), lax.axis_size("col")
    channels = wx.shape[-1]
    wide = 2 * channels
    x_shape = (nr, x_part.shape[0] // nr, MODES * wide)
    y_shape = (nc, y_part.shape[0] // nc, MODES * wide)
    dma = pltpu.SemaphoreType.DMA
    x_all, y_all = pl.pallas_call(
        functools.partial(exchange_kernel, nr, nc),
        out_shape=(
            jax.ShapeDtypeStruct(x_shape, jnp.bfloat16),
            jax.ShapeDtypeStruct(y_shape, jnp.bfloat16),
        ),
        in_specs=[pl.BlockSpec(memory_space=VMEM)] * 4,
        out_specs=(pl.BlockSpec(memory_space=VMEM),) * 2,
        scratch_shapes=[
            VMEM(x_shape, jnp.bfloat16),
            VMEM(y_shape, jnp.bfloat16),
            VMEM((MODES, wide, wide), jnp.bfloat16),
            VMEM((MODES, wide, wide), jnp.bfloat16),
            dma((nr,)), dma((nr,)), dma((nc,)), dma((nc,)),
            dma((nr,)), dma((nr,)), dma((nc,)), dma((nc,)),
        ],
        compiler_params=pltpu.CompilerParams(
            collective_id=0, has_side_effects=True, vmem_limit_bytes=32 << 20
        ),
        name="exchange",
    )(x_part.reshape(x_shape), y_part.reshape(y_shape), wx, wy)
    return (
        x_all.reshape(x_part.shape[0], 2 * MODES, channels),
        y_all.reshape(y_part.shape[0], 2 * MODES, channels),
    )


def feed_kernel(g_ref, up_ref, bias_ref, down_ref, out_ref):
    up = up_ref[...]
    bias = bias_ref[...]
    down = down_ref[...]
    for at in range(g_ref.shape[0]):
        block = g_ref[at]
        hidden = jnp.dot(up, block, preferred_element_type=jnp.float32) + bias
        hidden = (0.5 * hidden * (1.0 + lax.erf(hidden * math.sqrt(0.5)))).astype(jnp.bfloat16)
        back = jnp.dot(down, hidden, preferred_element_type=jnp.float32)
        out_ref[at] = (block.astype(jnp.float32) + back).astype(jnp.bfloat16)


def feed(gfield, up, bias, down):
    lines, channels, cols = gfield.shape
    step = math.gcd(lines, 4)
    units = up.shape[0]
    return pl.pallas_call(
        feed_kernel,
        grid=(lines // step,),
        out_shape=jax.ShapeDtypeStruct(gfield.shape, jnp.bfloat16),
        in_specs=[
            pl.BlockSpec((step, channels, cols), lambda i: (i, 0, 0)),
            pl.BlockSpec((units, channels), lambda i: (0, 0)),
            pl.BlockSpec((units, 1), lambda i: (0, 0)),
            pl.BlockSpec((channels, units), lambda i: (0, 0)),
        ],
        out_specs=pl.BlockSpec((step, channels, cols), lambda i: (i, 0, 0)),
        compiler_params=pltpu.CompilerParams(vmem_limit_bytes=32 << 20),
        name="feed",
    )(gfield, up, bias[:, None], down)


def on_device(field, x_weight, y_weight, up_weight, up_bias, down_weight):
    planes, channels, rows_here, cols_here = field.shape
    total_x = rows_here * lax.axis_size("row")
    total_y = cols_here * lax.axis_size("col")
    fwd_x, inv_x = tables(total_x, lax.axis_index("row") * rows_here, rows_here)
    fwd_y, inv_y = tables(total_y, lax.axis_index("col") * cols_here, cols_here)
    results = []
    for z in range(planes):
        state = field[z].transpose(1, 0, 2)
        for layer in range(LAYERS):
            x_part = jnp.einsum("mx,xcy->ymc", fwd_x, state, preferred_element_type=jnp.float32)
            y_part = jnp.einsum("my,xcy->xmc", fwd_y, state, preferred_element_type=jnp.float32)
            x_mixed, y_mixed = exchange(
                x_part.astype(jnp.bfloat16), y_part.astype(jnp.bfloat16),
                x_weight[layer], y_weight[layer],
            )
            back_x = jnp.einsum("mx,ymo->xoy", inv_x, x_mixed, preferred_element_type=jnp.float32)
            back_y = jnp.einsum("my,xmo->xoy", inv_y, y_mixed, preferred_element_type=jnp.float32)
            gfield = (state.astype(jnp.float32) + back_x + back_y).astype(jnp.bfloat16)
            state = feed(gfield, up_weight[layer], up_bias[layer], down_weight[layer])
        results.append(state.transpose(1, 0, 2))
    return jnp.stack(results)


def solution(mesh):
    in_specs = (P(None, None, "row", "col"), P(), P(), P(), P(), P())
    out_specs = P(None, None, "row", "col")
    return jax.shard_map(
        on_device, mesh=mesh, in_specs=in_specs, out_specs=out_specs, check_vma=False
    )
```

profile of v0, /device:TPU:0, one launch (start us, length us, event | category | flops | bytes accessed | tf_op | source)
XLA Modules:
  0.0 113.2 jit_solution(965229800843771629)
XLA Ops:
  0.0 0.2 fusion.21
  0.2 1.6 %fusion.4 = bf16[128,24,64]{0,1,2:T(8,128)(2,1)S(1)} fusion(bf16[24,64,1]{1,0,2:T(8,128)(2,1)S(1)} %bitcast.78, bf16[1,64,64,128]{3,2,1,0:T(8,128)(2,1)} %param.6), kind=kOutput, calls=%fused_computation.10 | convolution fusion | flops 25362432 | bytes 1444864 | tf_op jit(solution)/shard_map/mx,xcy->ymc/dot_general | solution.py:179
  1.8 0.5 copy.21
  2.3 0.5 reshape.350.x_in
  2.8 0.2 fusion.20
  3.0 1.0 fusion.5
  4.0 0.3 reshape.351.y_in
  4.3 3.1 %slice_bitcast_fusion = (f32[2,12,64,64]{3,2,1,0:T(8,128)S(1)}, f32[2,12,64,64]{3,2,1,0:T(8,128)S(1)}, f32[2,12,64,64]{3,2,1,0:T(8,128)S(1)}, f32[2,12,64,64]{3,2,1,0:T(8,128)}) fusion(f32[2,2,12,64,64]{4,3,2,1,0:T(8,128)} %param.8, f32[2,2,12,64,64]{4,3,2,1,0:T(8,128)} %param.7), kind=kLoop, calls=%fused_computation.18 | loop fusion | bytes 3145728 | tf_op jit(solution)/shard_map/squeeze | solution.py:183
  7.4 23.1 %exchange.2 = (bf16[8,16,1536]{2,1,0:T(8,128)(2,1)S(1)}, bf16[4,16,1536]{2,1,0:T(8,128)(2,1)S(1)}) custom-call(bf16[8,16,1536]{2,1,0:T(8,128)(2,1)S(1)} %reshape.350.x_in, bf16[4,16,1536]{2,1,0:T(8,128)(2,1)S(1)} %reshape.351.y_in, f32[2,12,64,64]{3,2,1,0:T(8,128)S(1)} %get-tuple-element.27.wx, f32[2,12,64,64]{3,2,1,0:T(8,128)S(1)} %get-tuple-element.14.wy), custom_call_target="tpu_custom_call" | custom-call | tf_op jit(solution)/shard_map/exchange/pallas_call | solution.py:110
  30.5 0.4 reshape.352
  31.0 2.7 %fusion.24 = f32[128,64,64]{2,1,0:T(8,128)} fusion(bf16[128,24,64]{2,1,0:T(8,128)(2,1)S(1)} %reshape.352, bf16[24,64,1]{1,0,2:T(8,128)(2,1)S(1)} %bitcast.84), kind=kOutput, calls=%fused_computation.53 | convolution fusion | flops 25165824 | bytes 2493440 | tf_op jit(solution)/shard_map/mx,ymo->xoy/dot_general | solution.py:185
  33.8 5.3 %copy.23 = f32[128,64,64]{0,1,2:T(8,128)} copy(f32[128,64,64]{2,1,0:T(8,128)} %fusion.24) | data formatting | bytes 4194304 | tf_op jit(solution)/shard_map/mx,ymo->xoy/dot_general | solution.py:185
  39.1 0.2 reshape.353
  39.4 2.8 %fusion.3.g_ref = bf16[64,64,128]{2,1,0:T(8,128)(2,1)S(1)} fusion(f32[128,64,64]{0,1,2:T(8,128)} %copy.23, bf16[64,24,64]{2,1,0:T(8,128)(2,1)S(1)} %reshape.353, bf16[24,128,1]{1,0,2:T(8,128)(2,1)S(1)} %bitcast.82, bf16[1,64,64,128]{3,2,1,0:T(8,128)(2,1)} %param.6), kind=kOutput, calls=%fused_computation.5 | convolution fusion | flops 27262976 | bytes 4397056 | tf_op jit(solution)/shard_map/my,xmo->xoy/dot_general | solution.py:186
  42.3 0.1 copy.25.bias_ref
  42.6 13.5 %feed.2 = bf16[64,64,128]{2,1,0:T(8,128)(2,1)S(1)} custom-call(bf16[64,64,128]{2,1,0:T(8,128)(2,1)S(1)} %fusion.3.g_ref, bf16[256,64]{1,0:T(8,128)(2,1)S(1)} %bitcast.76, f32[256,1]{1,0:T(8,128)S(1)} %copy.25.bias_ref, bf16[64,256]{1,0:T(8,128)(2,1)S(1)} %get-tuple-element.18.down_ref), custom_call_target="tpu_custom_call" | custom-call | tf_op jit(solution)/shard_map/feed/pallas_call | solution.py:153
  56.1 0.7 fusion.6
  56.8 1.4 %copy.27 = bf16[128,24,64]{2,1,0:T(8,128)(2,1)} copy(bf16[128,24,64]{0,1,2:T(8,128)(2,1)S(1)} %fusion.6) | data formatting | bytes 786432 | tf_op jit(solution)/shard_map/convert_element_type | solution.py:182
  58.1 1.8 %reshape.354.x_in = bf16[8,16,1536]{2,1,0:T(8,128)(2,1)S(1)} reshape(bf16[128,24,64]{2,1,0:T(8,128)(2,1)} %copy.27) | data formatting | bytes 786432 | tf_op jit(solution)/shard_map/reshape | solution.py:130
  59.9 1.7 %fusion.7 = bf16[64,24,64]{2,1,0:T(8,128)(2,1)} fusion(bf16[64,64,128]{2,1,0:T(8,128)(2,1)S(1)} %feed.2, bf16[24,128,1]{1,0,2:T(8,128)(2,1)S(1)} %bitcast.81), kind=kOutput, calls=%fused_computation.13 | convolution fusion | flops 25264128 | bytes 1251328 | tf_op jit(solution)/shard_map/my,xcy->xmc/dot_general | solution.py:180
  61.6 1.3 %reshape.355.y_in = bf16[4,16,1536]{2,1,0:T(8,128)(2,1)S(1)} reshape(bf16[64,24,64]{2,1,0:T(8,128)(2,1)} %fusion.7) | data formatting | bytes 393216 | tf_op jit(solution)/shard_map/reshape | solution.py:130
  62.9 22.2 %exchange.3 = (bf16[8,16,1536]{2,1,0:T(8,128)(2,1)S(1)}, bf16[4,16,1536]{2,1,0:T(8,128)(2,1)S(1)}) custom-call(bf16[8,16,1536]{2,1,0:T(8,128)(2,1)S(1)} %reshape.354.x_in, bf16[4,16,1536]{2,1,0:T(8,128)(2,1)S(1)} %reshape.355.y_in, f32[2,12,64,64]{3,2,1,0:T(8,128)S(1)} %copy-done, f32[2,12,64,64]{3,2,1,0:T(8,128)S(1)} %get-tuple-element.13.wy), custom_call_target="tpu_custom_call" | custom-call | tf_op jit(solution)/shard_map/exchange/pallas_call | solution.py:110
  85.1 0.7 copy-done.1
  85.9 1.6 %reshape.356 = bf16[128,24,64]{2,1,0:T(8,128)(2,1)S(1)} reshape(bf16[8,16,1536]{2,1,0:T(8,128)(2,1)} %copy-done.1) | data formatting | bytes 786432 | tf_op jit(solution)/shard_map/reshape | solution.py:132
  87.4 2.7 %fusion.25 = f32[128,64,64]{2,1,0:T(8,128)} fusion(bf16[128,24,64]{2,1,0:T(8,128)(2,1)S(1)} %reshape.356, bf16[24,64,1]{1,0,2:T(8,128)(2,1)S(1)} %bitcast.85), kind=kOutput, calls=%fused_computation.54 | convolution fusion | flops 25165824 | bytes 2493440 | tf_op jit(solution)/shard_map/mx,ymo->xoy/dot_general | solution.py:185
  90.1 5.3 %copy.29 = f32[128,64,64]{0,1,2:T(8,128)} copy(f32[128,64,64]{2,1,0:T(8,128)} %fusion.25) | data formatting | bytes 4194304 | tf_op jit(solution)/shard_map/mx,ymo->xoy/dot_general | solution.py:185
  95.4 0.2 reshape.357
  95.7 2.1 %fusion.1.g_ref = bf16[64,64,128]{2,1,0:T(8,128)(2,1)S(1)} fusion(f32[128,64,64]{0,1,2:T(8,128)} %copy.29, bf16[64,64,128]{2,1,0:T(8,128)(2,1)S(1)} %feed.2, bf16[64,24,64]{2,1,0:T(8,128)(2,1)S(1)} %reshape.357, bf16[24,128,1]{1,0,2:T(8,128)(2,1)S(1)} %bitcast.83), kind=kOutput, calls=%fused_computation.2 | convolution fusion | flops 27262976 | bytes 4397056 | tf_op jit(solution)/shard_map/my,xmo->xoy/dot_general | solution.py:186
  97.8 0.1 copy.31.bias_ref
  97.9 0.1 copy.41
  98.1 13.5 %feed.3 = bf16[64,64,128]{2,1,0:T(8,128)(2,1)S(1)} custom-call(bf16[64,64,128]{2,1,0:T(8,128)(2,1)S(1)} %fusion.1.g_ref, bf16[256,64]{1,0:T(8,128)(2,1)S(1)} %bitcast.77, f32[256,1]{1,0:T(8,128)S(1)} %copy.31.bias_ref, bf16[64,256]{1,0:T(8,128)(2,1)S(1)} %get-tuple-element.17.down_ref), custom_call_target="tpu_custom_call" | custom-call | tf_op jit(solution)/shard_map/feed/pallas_call | solution.py:153
  111.6 1.6 %copy.32 = bf16[1,64,64,128]{3,2,1,0:T(8,128)(2,1)} copy(bf16[1,64,64,128]{3,1,2,0:T(8,128)(2,1)S(1)} %bitcast.75) | data formatting | bytes 2097152 | tf_op jit(solution)/shard_map/stack | solution.py:190
  (22 shorter events, 0.4 us)
Async XLA Ops:
  0.0 3.0 %copy-start.2 = (bf16[1,64,64,128]{3,2,1,0:T(8,128)(2,1)S(1)}, bf16[1,64,64,128]{3,2,1,0:T(8,128)(2,1)}, u32[]{:S(2)}) copy-start(bf16[1,64,64,128]{3,2,1,0:T(8,128)(2,1)} %param.6) | copy-start | bytes 3145732
  39.4 2.9 %copy-start.5 = (f32[2,256]{1,0:T(2,128)S(1)}, f32[2,256]{1,0:T(2,128)}, u32[]{:S(2)}) copy-start(f32[2,256]{1,0:T(2,128)} %param.10) | copy-start | bytes 6148
  39.4 3.0 %copy-start.3 = (bf16[2,256,64]{1,2,0:T(8,128)(2,1)S(1)}, bf16[2,256,64]{1,2,0:T(8,128)(2,1)}, u32[]{:S(2)}) copy-start(bf16[2,256,64]{1,2,0:T(8,128)(2,1)} %param.9) | copy-start | bytes 196612
  39.4 3.2 %copy-start.4 = (bf16[2,64,256]{2,1,0:T(8,128)(2,1)S(1)}, bf16[2,64,256]{2,1,0:T(8,128)(2,1)}, u32[]{:S(2)}) copy-start(bf16[2,64,256]{2,1,0:T(8,128)(2,1)} %param.11) | copy-start | bytes 196612
  56.8 6.1 %copy-start = (f32[2,12,64,64]{3,2,1,0:T(8,128)S(1)}, f32[2,12,64,64]{3,2,1,0:T(8,128)}, u32[]{:S(2)}) copy-start(f32[2,12,64,64]{3,2,1,0:T(8,128)} %get-tuple-element.28.wx) | copy-start | bytes 1179652
  85.1 0.7 copy-start.1
where the time goes:
time: 113 us
  Pallas kernels  72.3 us (64%)
  local copies, waits for them, and re-layouts  24.7 us (22%)
  matrix products  15.3 us (14%)
    pallas_call x2, Pallas kernels, exchange(): pl.pallas_call(functools.partial(exchange_kernel, nr, nc), out_shape=(jax...  45.3 us
    pallas_call x2, Pallas kernels, feed(): pl.pallas_call(feed_kernel, grid=(lines // step,), out_shape=jax.ShapeDty...  27 us
    dot_general x2, local copies, waits for them, and re-layouts, on_device(): jnp.einsum('mx,ymo->xoy', inv_x, x_mixed, preferred_element_type=jnp.floa...  10.6 us
    dot_general x2, matrix products, on_device(): jnp.einsum('mx,ymo->xoy', inv_x, x_mixed, preferred_element_type=jnp.floa...  5.44 us
    dot_general x2, matrix products, on_device(): jnp.einsum('my,xmo->xoy', inv_y, y_mixed, preferred_element_type=jnp.floa...  4.94 us
    squeeze x1, local copies, waits for them, and re-layouts, on_device(): y_weight[layer]  3.09 us
    dot_general x2, matrix products, on_device(): jnp.einsum('my,xcy->xmc', fwd_y, state, preferred_element_type=jnp.float32)  2.63 us

commit v1 on v0

v1 whole, which is shorter than its diff:
```python
import functools
import math

import jax
import jax.numpy as jnp
from jax import lax
from jax.experimental import pallas as pl
from jax.experimental.pallas import tpu as pltpu
from jax.sharding import PartitionSpec as P

MODES = 12
LAYERS = 2
MESH = pl.DeviceIdType.MESH
VMEM = pltpu.VMEM


def tables(total, start, count):
    pos = start + jnp.arange(count, dtype=jnp.int32)
    kays = jnp.arange(MODES, dtype=jnp.int32)
    phase = kays[:, None] * pos[None, :] % total
    angle = phase.astype(jnp.float32) * (2.0 * math.pi / total)
    both = jnp.stack([jnp.cos(angle), -jnp.sin(angle)], axis=1)
    factor = (jnp.where(kays == 0, 1.0, 2.0) / total).astype(jnp.float32)[:, None, None]
    forward = both.astype(jnp.bfloat16).reshape(2 * MODES, count)
    inverse = (both * factor).astype(jnp.bfloat16).reshape(2 * MODES, count)
    return forward, inverse


def exchange_kernel(
    nr, nc, layer, x_in, y_in, wx, wy, x_out, y_out, x_got, y_got, x_w, y_w, x_mat, y_mat,
    w_sem, xs_send, xs_recv, ys_send, ys_recv, xg_send, xg_recv, yg_send, yg_recv,
):
    row = lax.axis_index("row")
    col = lax.axis_index("col")

    def row_peer(d):
        return (lax.rem(row + d, nr), col)

    def col_peer(d):
        return (row, lax.rem(col + d, nc))

    y_load = pltpu.make_async_copy(wy.at[layer], y_w, w_sem.at[0])
    x_load = pltpu.make_async_copy(wx.at[layer], x_w, w_sem.at[1])
    y_load.start()
    x_load.start()

    barrier = pltpu.get_barrier_semaphore()
    for d in range(1, nr):
        pl.semaphore_signal(barrier, inc=1, device_id=row_peer(d), device_id_type=MESH)
    for d in range(1, nc):
        pl.semaphore_signal(barrier, inc=1, device_id=col_peer(d), device_id_type=MESH)
    pl.semaphore_wait(barrier, nr + nc - 2)

    def copy(src, dst, send, recv, d, peer):
        made = pltpu.make_async_remote_copy(
            src_ref=src, dst_ref=dst, send_sem=send.at[d], recv_sem=recv.at[d],
            device_id=peer, device_id_type=MESH,
        )
        made.start()
        return made

    x_scatter = [
        copy(x_in.at[row_peer(d)[0]], x_got.at[d], xs_send, xs_recv, d, row_peer(d))
        for d in range(1, nr)
    ]
    y_scatter = [
        copy(y_in.at[col_peer(d)[1]], y_got.at[d], ys_send, ys_recv, d, col_peer(d))
        for d in range(1, nc)
    ]

    for load, w, mat in ((y_load, y_w, y_mat), (x_load, x_w, x_mat)):
        load.wait()
        for k in range(MODES):
            real = w[0, k]
            imag = w[1, k]
            top = jnp.concatenate([real, imag], axis=1)
            bottom = jnp.concatenate([-imag, real], axis=1)
            mat[k] = jnp.concatenate([top, bottom], axis=0).astype(jnp.bfloat16)

    def mix(own, first, got, n, mat, out):
        for k in range(MODES):
            total = first[own, k].astype(jnp.float32)
            for d in range(1, n):
                total = total + got[d, k].astype(jnp.float32)
            out[own, k] = jnp.dot(
                total.astype(jnp.bfloat16), mat[k], preferred_element_type=jnp.float32
            ).astype(jnp.bfloat16)

    for made in y_scatter:
        made.wait()
    mix(col, y_in, y_got, nc, y_mat, y_out)
    y_gather = [
        copy(y_out.at[col], y_out.at[col], yg_send, yg_recv, d, col_peer(d))
        for d in range(1, nc)
    ]
    for made in x_scatter:
        made.wait()
    mix(row, x_in, x_got, nr, x_mat, x_out)
    x_gather = [
        copy(x_out.at[row], x_out.at[row], xg_send, xg_recv, d, row_peer(d))
        for d in range(1, nr)
    ]
    for made in y_gather + x_gather:
        made.wait()


def exchange(x_part, y_part, wx, wy, layer):
    nr, nc = lax.axis_size("row"), lax.axis_size("col")
    wide = x_part.shape[-1]
    dma = pltpu.SemaphoreType.DMA
    whole = pl.BlockSpec(memory_space=VMEM)
    return pl.pallas_call(
        functools.partial(exchange_kernel, nr, nc, layer),
        out_shape=(
            jax.ShapeDtypeStruct(x_part.shape, jnp.bfloat16),
            jax.ShapeDtypeStruct(y_part.shape, jnp.bfloat16),
        ),
        in_specs=[whole, whole] + [pl.BlockSpec(memory_space=pl.ANY)] * 2,
        out_specs=(whole, whole),
        scratch_shapes=[
            VMEM(x_part.shape, jnp.bfloat16),
            VMEM(y_part.shape, jnp.bfloat16),
            VMEM(wx.shape[1:], jnp.float32),
            VMEM(wy.shape[1:], jnp.float32),
            VMEM((MODES, wide, wide), jnp.bfloat16),
            VMEM((MODES, wide, wide), jnp.bfloat16),
            dma((2,)),
            dma((nr,)), dma((nr,)), dma((nc,)), dma((nc,)),
            dma((nr,)), dma((nr,)), dma((nc,)), dma((nc,)),
        ],
        compiler_params=pltpu.CompilerParams(
            collective_id=layer, has_side_effects=True, vmem_limit_bytes=32 << 20
        ),
        name="exchange",
    )(x_part, y_part, wx, wy)


def dot(a, b, contract=((1,), (0,))):
    return lax.dot_general(a, b, (contract, ((), ())), preferred_element_type=jnp.float32)


def y_modes(line, state, fyc, fys, y_rows, lines):
    both = ((1,), (1,))
    parts = jnp.concatenate([dot(fyc, state, both), dot(fys, state, both)], axis=1)
    y_rows[pl.ds(line, MODES, stride=lines), :] = parts


def put_parts(x_rows, y_rows, x_part, y_part):
    nr, _, x_own, wide = x_part.shape
    nc, _, y_own, _ = y_part.shape
    for k in range(MODES):
        turned = x_rows[k * wide:(k + 1) * wide, :].T
        for i in range(nr):
            x_part[i, k] = turned[i * x_own:(i + 1) * x_own].astype(jnp.bfloat16)
        for i in range(nc):
            at = k * nc * y_own + i * y_own
            y_part[i, k] = y_rows[at:at + y_own, :].astype(jnp.bfloat16)


def start_kernel(field, fx, fyc, fys, state, x_part, y_part, big, x_rows, y_rows):
    channels, lines, _ = field.shape
    for c in range(channels):
        plane = field[c]
        x_rows[pl.ds(c, 2 * MODES, stride=channels), :] = dot(fx[...], plane)
        big[pl.ds(c, lines, stride=channels), :] = plane.astype(jnp.float32)

    def body(x, carry):
        here = big[pl.ds(pl.multiple_of(x * channels, channels), channels), :].astype(jnp.bfloat16)
        state[x] = here
        y_modes(x, here, fyc[...], fys[...], y_rows, lines)
        return carry

    lax.fori_loop(0, lines, body, 0, unroll=4)
    put_parts(x_rows, y_rows, x_part, y_part)


def layer_kernel(last, state, x_mixed, y_mixed, gx, gyc, gys, up, bias, down, *rest):
    if last:
        out, big, x_rows, y_rows, flat = rest
    else:
        fx, fyc, fys, out, x_part, y_part, big, x_rows, y_rows, flat = rest
    lines, channels, cols = state.shape
    both = 2 * MODES
    nr, _, x_own, _ = x_mixed.shape
    nc, _, y_own, _ = y_mixed.shape
    for k in range(MODES):
        for i in range(nr):
            flat[k, i * x_own:(i + 1) * x_own, :] = x_mixed[i, k].astype(jnp.float32)
        for i in range(nc):
            at = k * lines + i * y_own
            y_rows[at:at + y_own, :] = y_mixed[i, k].astype(jnp.float32)
    for k in range(MODES):
        turned = flat[k].T
        for part in range(2):
            x_rows[pl.ds(2 * k + part, channels, stride=both), :] = turned[
                part * channels:(part + 1) * channels
            ]
    for o in range(channels):
        modes = x_rows[o * both:(o + 1) * both, :].astype(jnp.bfloat16)
        big[pl.ds(o, lines, stride=channels), :] = dot(gx[...], modes)

    def body(x, carry):
        here = pl.ds(pl.multiple_of(x * channels, channels), channels)
        turned = y_rows[pl.ds(x, MODES, stride=lines), :].T.astype(jnp.bfloat16)
        back_y = dot(turned[:channels], gyc[...]) + dot(turned[channels:], gys[...])
        gline = (state[x].astype(jnp.float32) + big[here, :] + back_y).astype(jnp.bfloat16)
        hidden = dot(up[...], gline) + bias[...]
        hidden = (0.5 * hidden * (1.0 + lax.erf(hidden * math.sqrt(0.5)))).astype(jnp.bfloat16)
        fresh = gline.astype(jnp.float32) + dot(down[...], hidden)
        if last:
            big[here, :] = fresh
        else:
            rounded = fresh.astype(jnp.bfloat16)
            big[here, :] = rounded.astype(jnp.float32)
            out[x] = rounded
            y_modes(x, rounded, fyc[...], fys[...], y_rows, lines)
        return carry

    lax.fori_loop(0, lines, body, 0, unroll=2)
    for c in range(channels):
        plane = big[pl.ds(c, lines, stride=channels), :].astype(jnp.bfloat16)
        if last:
            out[c] = plane
        else:
            x_rows[pl.ds(c, both, stride=channels), :] = dot(fx[...], plane)
    if not last:
        put_parts(x_rows, y_rows, x_part, y_part)


def local_call(kernel, name, out_shape, scratch, *args):
    whole = pl.BlockSpec(memory_space=VMEM)
    return pl.pallas_call(
        kernel,
        out_shape=out_shape,
        in_specs=[whole] * len(args),
        out_specs=jax.tree.map(lambda _: whole, out_shape),
        scratch_shapes=[VMEM(shape, jnp.float32) for shape in scratch],
        compiler_params=pltpu.CompilerParams(vmem_limit_bytes=32 << 20),
        name=name,
    )(*args)


def on_device(field, x_weight, y_weight, up_weight, up_bias, down_weight):
    planes, channels, lines, cols = field.shape
    nr, nc = lax.axis_size("row"), lax.axis_size("col")
    fx, gx = tables(lines * nr, lax.axis_index("row") * lines, lines)
    fy, gy = tables(cols * nc, lax.axis_index("col") * cols, cols)
    gx = gx.T
    fyc, fys, gyc, gys = fy[0::2], fy[1::2], gy[0::2], gy[1::2]
    half = jnp.bfloat16
    state_shape = jax.ShapeDtypeStruct((lines, channels, cols), half)
    x_shape = jax.ShapeDtypeStruct((nr, MODES, cols // nr, 2 * channels), half)
    y_shape = jax.ShapeDtypeStruct((nc, MODES, lines // nc, 2 * channels), half)
    scratch = [(lines * channels, cols), (2 * MODES * channels, cols), (MODES * lines, 2 * channels)]
    more = scratch + [(MODES, cols, 2 * channels)]
    results = []
    for z in range(planes):
        state, x_part, y_part = local_call(
            start_kernel, "start", (state_shape, x_shape, y_shape), scratch, field[z], fx, fyc, fys
        )
        for layer in range(LAYERS):
            last = layer == LAYERS - 1
            x_mixed, y_mixed = exchange(x_part, y_part, x_weight, y_weight, layer)
            args = (
                state, x_mixed, y_mixed, gx, gyc, gys,
                up_weight[layer], up_bias[layer][:, None], down_weight[layer],
            )
            kernel = functools.partial(layer_kernel, last)
            if last:
                shape = jax.ShapeDtypeStruct((channels, lines, cols), half)
                results.append(local_call(kernel, "finish", shape, more, *args))
            else:
                state, x_part, y_part = local_call(
                    kernel, "layer", (state_shape, x_shape, y_shape), more, *args, fx, fyc, fys
                )
    return jnp.stack(results)


def solution(mesh):
    in_specs = (P(None, None, "row", "col"), P(), P(), P(), P(), P())
    out_specs = P(None, None, "row", "col")
    return jax.shard_map(
        on_device, mesh=mesh, in_specs=in_specs, out_specs=out_specs, check_vma=False
    )
```

time: 113 us -> 146 us (1.29)
  Pallas kernels: 72.3 us -> 121 us
  matrix products: 15.3 us -> 0 us
    pallas_call x4 -> x5, Pallas kernels: 72.3 us -> 121 us  [the longest x3 75.1 us: local_call(): pl.pallas_call(kernel, out_shape=out_shape, in_specs=[whole] * len(args),...]
    unnamed x14 -> x54, local copies, waits for them, and re-layouts: 1 us -> 18 us
    dot_general x8 -> x0, matrix products: 15.3 us -> none  [the longest x2 5.44 us: on_device(): jnp.einsum('mx,ymo->xoy', inv_x, x_mixed, preferred_element_type=jnp.floa...]
    dot_general x2 -> x0, local copies, waits for them, and re-layouts: 10.6 us -> none  [on_device(): jnp.einsum('mx,ymo->xoy', inv_x, x_mixed, preferred_element_type=jnp.floa...]
    reshape x8 -> x0, local copies, waits for them, and re-layouts: 6.25 us -> none  [the longest x2 2.23 us: exchange(): x_part.reshape(x_shape)]
    slice x1 -> x5, local copies, waits for them, and re-layouts: 0.01 us -> 1.92 us  [the longest x4 1.28 us: on_device(): fyc, fys, gyc, gys = (fy[0::2], fy[1::2], gy[0::2], gy[1::2])]
    convert_element_type x2 -> x0, local copies, waits for them, and re-layouts: 1.86 us -> none  [on_device(): x_part.astype(jnp.bfloat16)]
    squeeze x2 -> x1, local copies, waits for them, and re-layouts: 3.1 us -> 1.4 us  [on_device(): down_weight[layer]]
where the time goes in v1:
time: 146 us; the launch traced here: 145 us
  Pallas kernels  121 us (83%)
  local copies, waits for them, and re-layouts  23.7 us (16%)
    pallas_call x3, Pallas kernels, local_call(): pl.pallas_call(kernel, out_shape=out_shape, in_specs=[whole] * len(args),...  75.1 us
    pallas_call x2, Pallas kernels, exchange(): pl.pallas_call(functools.partial(exchange_kernel, nr, nc, layer), out_sha...  45.7 us
    unnamed x54, local copies, waits for them, and re-layouts  18 us

profile of v1, /device:TPU:0, one launch (start us, length us, event | category | flops | bytes accessed | tf_op | source)
XLA Modules:
  0.0 145.3 jit_solution(5893814708515783908)
XLA Ops:
  0.6 1.2 copy-done.6
  1.8 6.5 %start.1 = (bf16[64,64,128]{2,1,0:T(8,128)(2,1)S(1)}, bf16[8,12,16,128]{3,2,1,0:T(8,128)(2,1)S(1)}, bf16[4,12,16,128]{3,2,1,0:T(8,128)(2,1)S(1)}) custom-call(bf16[64,64,128]{2,1,0:T(8,128)(2,1)S(1)} %bitcast.16, bf16[24,64]{1,0:T(8,128)(2,1)S(1)} %convert_element_type.45.fx.rest_0_, bf16[12,128]{1,0:T(8,128)(2,1)S(1)} %slice.30.fyc.rest_1_, ...), custom_call_target="tpu_custom_call" | custom-call | tf_op jit(solution)/shard_map/start/pallas_call | solution.py:232
  8.3 1.0 copy-done.7
  9.3 1.4 copy-done
  10.7 1.4 copy-done.2
  12.1 23.3 %exchange.2 = (bf16[8,12,16,128]{3,2,1,0:T(8,128)(2,1)S(1)}, bf16[4,12,16,128]{3,2,1,0:T(8,128)(2,1)S(1)}) custom-call(bf16[8,12,16,128]{3,2,1,0:T(8,128)(2,1)S(1)} %get-tuple-element.16.x_in, bf16[4,12,16,128]{3,2,1,0:T(8,128)(2,1)S(1)} %get-tuple-element.17.y_in, f32[2,2,12,64,64]{4,3,2,1,0:T(8,128)S(1)} %copy-done, f32[2,2,12,64,64]{4,3,2,1,0:T(8,128)S(1)} %copy-done.2), custom_call_target="tpu_custom_call" | custom-call | tf_op jit(solution)/shard_map/exchange/pallas_call | solution.py:112
  35.5 0.7 copy-done.9
  36.4 0.6 slice.32.gyc
  37.1 0.6 slice.33.gys
  37.8 0.6 slice_bitcast_fusion.2
  38.3 0.8 copy.19.bias
  39.1 0.6 fusion.10
  39.8 0.9 copy.22
  40.6 1.4 slice_bitcast_fusion
  42.0 1.2 copy-done.8
  43.3 1.0 copy-done.10
  44.3 0.7 copy-done.15
  45.0 0.7 copy-done.17
  45.6 0.7 copy-done.19
  46.3 0.7 copy-done.20
  47.0 0.7 copy-done.22
  47.7 41.7 %layer.1 = (bf16[64,64,128]{2,1,0:T(8,128)(2,1)S(1)}, bf16[8,12,16,128]{3,2,1,0:T(8,128)(2,1)S(1)}, bf16[4,12,16,128]{3,2,1,0:T(8,128)(2,1)S(1)}) custom-call(bf16[64,64,128]{2,1,0:T(8,128)(2,1)S(1)} %copy-done.8, bf16[8,12,16,128]{3,2,1,0:T(8,128)(2,1)S(1)} %copy-done.10, bf16[4,12,16,128]{3,2,1,0:T(8,128)(2,1)S(1)} %get-tuple-element.19.y_mixed, ...), custom_call_target="tpu_custom_call" | custom-call | tf_op jit(solution)/shard_map/layer/pallas_call | solution.py:232
  89.4 22.4 %exchange.3 = (bf16[8,12,16,128]{3,2,1,0:T(8,128)(2,1)S(1)}, bf16[4,12,16,128]{3,2,1,0:T(8,128)(2,1)S(1)}) custom-call(bf16[8,12,16,128]{3,2,1,0:T(8,128)(2,1)S(1)} %get-tuple-element.21.x_in, bf16[4,12,16,128]{3,2,1,0:T(8,128)(2,1)S(1)} %get-tuple-element.22.y_in, f32[2,2,12,64,64]{4,3,2,1,0:T(8,128)S(1)} %copy-done.1, f32[2,2,12,64,64]{4,3,2,1,0:T(8,128)S(1)} %copy-done.3), custom_call_target="tpu_custom_call" | custom-call | tf_op jit(solution)/shard_map/exchange/pallas_call | solution.py:112
  111.8 0.7 copy-done.11
  112.4 0.8 copy.21.bias
  113.2 0.9 copy.23
  114.1 1.2 copy-done.5
  115.3 0.9 copy-done.12
  116.3 0.8 copy-done.13
  117.0 0.7 copy-done.21
  117.7 0.7 copy-done.23
  118.4 26.9 %finish.1 = bf16[64,64,128]{2,1,0:T(8,128)(2,1)} custom-call(bf16[64,64,128]{2,1,0:T(8,128)(2,1)S(1)} %copy-done.5, bf16[8,12,16,128]{3,2,1,0:T(8,128)(2,1)S(1)} %get-tuple-element.23.x_mixed, bf16[4,12,16,128]{3,2,1,0:T(8,128)(2,1)S(1)} %copy-done.12, bf16[64,24]{1,0:T(8,128)(2,1)S(1)} %fusion.gx, bf16[12,128]{1,0:T(8,128)(2,1)S(1)} %copy-done.21, ...), custom_call_target="tpu_custom_call" | custom-call | tf_op jit(solution)/shard_map/finish/pallas_call | solution.py:232
  (50 shorter events, 0.9 us)
Async XLA Ops:
  0.3 9.0 %copy-start.16 = (bf16[12,128]{1,0:T(8,128)(2,1)}, bf16[12,128]{1,0:T(8,128)(2,1)S(1)}, u32[]{:S(2)}) copy-start(bf16[12,128]{1,0:T(8,128)(2,1)S(1)} %slice.30.fyc.rest_1_) | copy-start | bytes 9220
  0.3 9.0 %copy-start.18 = (bf16[12,128]{1,0:T(8,128)(2,1)}, bf16[12,128]{1,0:T(8,128)(2,1)S(1)}, u32[]{:S(2)}) copy-start(bf16[12,128]{1,0:T(8,128)(2,1)S(1)} %slice.31.fys.rest_2_) | copy-start | bytes 9220
  0.5 8.7 %copy-start.14 = (bf16[24,64]{1,0:T(8,128)(2,1)}, bf16[24,64]{1,0:T(8,128)(2,1)S(1)}, u32[]{:S(2)}) copy-start(bf16[24,64]{1,0:T(8,128)(2,1)S(1)} %convert_element_type.45.fx.rest_0_) | copy-start | bytes 9220
  0.6 1.2 copy-start.6
  8.3 1.0 copy-start.7
  9.3 1.4 copy-start
  10.7 1.4 copy-start.2
  12.1 25.7 %copy-start.25 = (f32[2,256]{1,0:T(2,128)S(1)}, f32[2,256]{1,0:T(2,128)}, u32[]{:S(2)}) copy-start(f32[2,256]{1,0:T(2,128)} %param.10) | copy-start | bytes 6148
  12.1 27.0 %copy-start.24 = (bf16[2,256,64]{1,2,0:T(8,128)(2,1)S(1)}, bf16[2,256,64]{1,2,0:T(8,128)(2,1)}, u32[]{:S(2)}) copy-start(bf16[2,256,64]{1,2,0:T(8,128)(2,1)} %param.9) | copy-start | bytes 196612
  12.1 77.2 %copy-start.3 = (f32[2,2,12,64,64]{4,3,2,1,0:T(8,128)S(1)}, f32[2,2,12,64,64]{4,3,2,1,0:T(8,128)}, u32[]{:S(2)}) copy-start(f32[2,2,12,64,64]{4,3,2,1,0:T(8,128)} %wy.3) | copy-start | bytes 2359300
  35.5 0.7 copy-start.9
  36.2 53.2 %copy-start.1 = (f32[2,2,12,64,64]{4,3,2,1,0:T(8,128)S(1)}, f32[2,2,12,64,64]{4,3,2,1,0:T(8,128)}, u32[]{:S(2)}) copy-start(f32[2,2,12,64,64]{4,3,2,1,0:T(8,128)} %wx.3) | copy-start | bytes 2359300
  42.0 1.2 copy-start.8
  43.3 1.0 copy-start.10
  44.3 0.7 copy-start.15
  44.9 0.7 copy-start.17
  45.6 0.7 copy-start.19
  46.3 0.7 copy-start.20
  47.0 0.7 copy-start.22
  89.3 22.4 %copy-start.4 = (bf16[64,64,128]{2,1,0:T(8,128)(2,1)}, bf16[64,64,128]{2,1,0:T(8,128)(2,1)S(1)}, u32[]{:S(2)}) copy-start(bf16[64,64,128]{2,1,0:T(8,128)(2,1)S(1)} %get-tuple-element.20.state) | copy-start | bytes 3145732
  111.7 0.7 copy-start.11
  114.1 1.2 copy-start.5
  115.3 0.9 copy-start.12
  116.3 0.8 copy-start.13
  117.0 0.7 copy-start.21
  117.7 0.7 copy-start.23
